TPU v7x, 256 devices: a whole 4x4x8 slice. The times are simulated.
256 devices in a mesh: section: 8 (over z), shard: 32 (over x, y, core).
Axes of the slice: x: 4, y: 4, z: 8, core: 2. Of those that a mesh axis runs over, the one named last changes fastest.
Arguments:
- deltas: bfloat16 [8, 2, 256, 8192], P('section', None, 'shard'), may hold values from -30 to 30, as said below
- backs: bfloat16 [8, 2, 256, 8192], P('section', None, 'shard'), may hold values from -6 to 6
- gains: float32 [8, 8192], P('section'), may hold values from 0.25 to 1.75
Outputs:
- act_cov: bfloat16 [8, 8192, 8192], P('section', 'shard')
- grad_cov: bfloat16 [8, 8192, 8192], P('section', 'shard')
Inputs may be any that keep to these rules, and one draw needn't show every extreme that they name: `deltas`: entries of the section terms, rows and columns of differing scales.
All inputs are finite; a program needn't handle non-finite values.
Results may differ from a plain program's by a relative error of at most 0.0057.
Values may be sent and summed in bfloat16 or wider, within the bound.
A program may use at most 64 MiB of HBM per device.

v0:
```python
import jax
import jax.numpy as jnp
from jax import lax
from jax.sharding import PartitionSpec as P

EPSILON = 1e-05


def side_by_side(arrays, axis, dim, along):
    ends, at = ([], 0)
    for a in arrays[:-1]:
        at += a.shape[along]
        ends.append(at)
    both = jnp.concatenate(arrays, axis=along)
    return tuple(jnp.split(lax.all_gather(both, axis, axis=dim, tiled=True), ends, axis=along))


def collected_sums(own_fwd, own_bwd):
    every_fwd, every_bwd = side_by_side(
        (own_fwd.astype(jnp.bfloat16)[None], own_bwd.astype(jnp.bfloat16)[None]), "section", 0, 1
    )
    section_count = every_fwd.shape[0]
    my_section = lax.axis_index("section")
    section_ids = jnp.arange(section_count, dtype=jnp.int32).reshape(
        (section_count,) + (1,) * own_fwd.ndim
    )
    forward = jnp.sum(
        jnp.where(section_ids <= my_section, every_fwd.astype(jnp.float32), 0.0), axis=0
    )
    backward = jnp.sum(
        jnp.where(section_ids >= my_section, every_bwd.astype(jnp.float32), 0.0), axis=0
    )
    return (forward, backward)


def accumulate(totals, own_fwd, own_bwd, gain_row):
    forward, backward = collected_sums(own_fwd, own_bwd)
    model_width = forward.shape[-1]
    inverse = lax.rsqrt(jnp.mean(forward * forward, axis=-1, keepdims=True) + EPSILON)
    normed = (forward * inverse * gain_row).astype(jnp.bfloat16).reshape(-1, model_width)
    grad_bf = backward.astype(jnp.bfloat16).reshape(-1, model_width)
    tile_rows = totals[0].shape[0]
    own_start = lax.axis_index("shard") * tile_rows
    contract = (((0,), (0,)), ((), ()))
    act_rows, grad_rows = side_by_side((normed, grad_bf), "shard", 0, 1)
    left_act = lax.dynamic_slice_in_dim(act_rows, own_start, tile_rows, 1)
    left_grad = lax.dynamic_slice_in_dim(grad_rows, own_start, tile_rows, 1)
    act_part = lax.dot_general(left_act, act_rows, contract, preferred_element_type=jnp.float32)
    grad_part = lax.dot_general(left_grad, grad_rows, contract, preferred_element_type=jnp.float32)
    return (act_part, grad_part)


def shards(deltas, backs, gains):
    model_width = deltas.shape[-1]
    tile_rows = model_width // lax.axis_size("shard")
    gain_row = gains[0]
    empty_tile = jnp.zeros((tile_rows, model_width), jnp.float32)
    totals = (empty_tile, empty_tile)
    totals = accumulate(
        totals, deltas[0].astype(jnp.float32), backs[0].astype(jnp.float32), gain_row
    )
    token_count = deltas.shape[1] * deltas.shape[2] * lax.axis_size("shard")
    act_cov = (totals[0] / token_count).astype(jnp.bfloat16)[None]
    grad_cov = (totals[1] / token_count).astype(jnp.bfloat16)[None]
    return (act_cov, grad_cov)


def solution(mesh):
    return jax.shard_map(
        shards,
        mesh=mesh,
        in_specs=(
            P("section", None, "shard", None),
            P("section", None, "shard", None),
            P("section", None),
        ),
        out_specs=(P("section", "shard", None), P("section", "shard", None)),
        check_vma=False,
    )
```

profile of v0, /device:TPU:97, one launch (start us, length us, event | category | flops | bytes accessed | tf_op | source)
XLA Modules:
  0.0 171.5 jit_solution(4467955383758116105)
XLA Ops:
  7.2 0.0 all-gather.3.cloned.1.call-start
  7.2 1.9 %pad_maximum_fusion = bf16[1,4,8,8192]{3,2,1,0:T(8,128)(2,1)} fusion(bf16[1,2,8,8192]{3,2,1,0:T(8,128)(2,1)} %param.4, bf16[1,2,8,8192]{3,2,1,0:T(8,128)(2,1)} %param.3), kind=kLoop, calls=%fused_computation.8 | loop fusion | flops 262144 | bytes 1048576 | tf_op jit(solution)/shard_map/concatenate | solution.py:14
  9.1 0.0 all-gather.3.cloned.1.call-update
  9.1 0.0 all-gather.5.cloned.1.call-start
  9.2 57.3 %all-gather.3.cloned.1.call-done = bf16[8,4,8,8192]{3,2,1,0:T(8,128)(2,1)} async-done(((bf16[1,4,8,8192]{3,2,1,0:T(8,128)(2,1)}), bf16[8,4,8,8192]{3,2,1,0:T(8,128)(2,1)}) %all-gather.3.cloned.1.call-update) | async-done | bytes 4194320 | tf_op jit(solution)/shard_map/all_gather | solution.py:15
  66.5 3.2 %select_reduce_fusion.1 = (f32[2,8,8192]{2,1,0:T(8,128)S(1)}, bf16[2,8,8192]{2,1,0:T(8,128)(2,1)S(1)}) fusion(bf16[8,4,8,8192]{3,2,1,0:T(8,128)(2,1)} %all-gather.3.cloned.1.call-done, pred[8]{0:T(512)(128)(4,1)S(1)} %get-tuple-element.7, pred[8]{0:T(512)(128)(4,1)S(1)} %get-tuple-element.6), kind=kLoop, calls=%fused_computation.7 | loop fusion | flops 6029312 | bytes 4980752 | tf_op jit(solution)/shard_map/reduce_sum | solution.py:27
  69.7 0.2 multiply_reduce_fusion
  69.9 0.1 rsqrt.12
  69.9 0.9 fusion.5
  70.8 0.8 pad_maximum_fusion.1
  71.6 0.0 all-gather.5.cloned.1.call-update
  71.7 77.3 %all-gather.5.cloned.1.call-done = bf16[512,16384]{1,0:T(8,128)(2,1)} async-done(((bf16[16,16384]{1,0:T(8,128)(2,1)}), bf16[512,16384]{1,0:T(8,128)(2,1)}) %all-gather.5.cloned.1.call-update) | async-done | bytes 16777232 | tf_op jit(solution)/shard_map/all_gather | solution.py:15
  148.9 6.7 %fusion.10 = (bf16[512,8192]{1,0:T(8,128)(2,1)S(1)}, bf16[512,8192]{1,0:T(8,128)(2,1)S(1)}) fusion(bf16[512,16384]{1,0:T(8,128)(2,1)} %all-gather.5.cloned.1.call-done), kind=kLoop, calls=%fused_computation.22 | loop fusion | bytes 33554432 | tf_op jit(solution)/shard_map/split | solution.py:15
  155.6 4.5 %fusion.2 = bf16[1,256,8192]{2,1,0:T(8,128)(2,1)} fusion(bf16[512,8192]{1,0:T(8,128)(2,1)S(1)} %get-tuple-element.4, s32[]{:T(128)S(6)} %select_n.13), kind=kOutput, calls=%fused_computation.4 | convolution fusion | flops 2151677952 | bytes 12845060 | tf_op jit(solution)/shard_map/dot_general | solution.py:49
  160.1 4.5 %fusion.3 = bf16[1,256,8192]{2,1,0:T(8,128)(2,1)} fusion(bf16[512,8192]{1,0:T(8,128)(2,1)S(1)} %get-tuple-element.5, s32[]{:T(128)S(6)} %select_n.13), kind=kOutput, calls=%fused_computation.5 | convolution fusion | flops 2151677952 | bytes 12845060 | tf_op jit(solution)/shard_map/dot_general | solution.py:48
  (2 shorter events, 0.0 us)
Async XLA Ops:
  7.2 59.4 %all-gather.3.cloned.1.call-start = ((), (), s32[]{:S(2)}) async-start(), calls=%async_computation | async-start | bytes 4718592 | tf_op jit(solution)/shard_map/all_gather | solution.py:15
  9.1 139.8 %all-gather.5.cloned.1.call-start = ((), (), s32[]{:S(2)}) async-start(), calls=%async_computation.1 | async-start | bytes 17301504 | tf_op jit(solution)/shard_map/all_gather | solution.py:15
Sparse Core Ops, SparseCore 0:
  10.4 56.1 all-gather.2
  71.8 77.0 all-gather.4
where the time goes:
time: 174 us; the launch traced here: 171 us
  waiting for transfers between devices  135 us (78%)
  between operations  14.1 us (8%)
  matrix products  9.05 us (5%)
  other arithmetic  6.92 us (4%)
  local copies, waits for them, and re-layouts  6.75 us (4%)
    all_gather x2, waiting for transfers between devices, side_by_side(): lax.all_gather(both, axis, axis=dim, tiled=True)  135 us
    split x1, local copies, waits for them, and re-layouts, side_by_side(): jnp.split(lax.all_gather(both, axis, axis=dim, tiled=True), ends, axis=al...  6.67 us
    dot_general x1, matrix products, accumulate(): lax.dot_general(left_grad, grad_rows, contract, preferred_element_type=jn...  4.53 us
    dot_general x1, matrix products, accumulate(): lax.dot_general(left_act, act_rows, contract, preferred_element_type=jnp....  4.52 us
  transfers between devices with their start and end apart: 2, of which 2 were waited for; matrix products, arithmetic and copies ran while one was open for 0% of the time, Pallas kernels for 0%

commit v1 on v0

v1 whole, which is shorter than its diff:
```python
import functools
import jax
import jax.numpy as jnp
from jax import lax
from jax.experimental import pallas as pl
from jax.experimental.pallas import tpu as pltpu
from jax.sharding import PartitionSpec as P

EPSILON = 1e-05
CHUNKS = 4
RING = 4
PLANE = RING * RING
SENDS = 36
ORDER = (0, 3, 1, 2)


def slot(da, db):
    return da * RING + db


def plane_copies():
    copies = {}
    copies["a+", 0] = (slot(0, 0), slot(3, 0), None, "a+")
    copies["a-", 0] = (slot(0, 0), slot(1, 0), None, "a-")
    copies["a+", 1] = (slot(3, 0), slot(2, 0), 0, "a+")
    copies["a-", 1] = (slot(1, 0), slot(2, 0), 1, "a-")
    for da in ORDER:
        copies["b+", da, 0] = (slot(da, 0), slot(da, 3), None, "b+")
        copies["b-", da, 0] = (slot(da, 0), slot(da, 1), None, "b-")
        copies["b+", da, 1] = (slot(da, 3), slot(da, 2), 0, "b+")
        copies["b-", da, 1] = (slot(da, 1), slot(da, 2), 1, "b-")
    for at in range(PLANE):
        copies["s", at] = (at, PLANE + at, None, "s")
    return copies


def gather_kernel(deltas, backs, gains, g, inp, zbuf, in_sem, zsend, zrecv, send, recv):
    width = inp.shape[-1]
    part = width // CHUNKS
    half_width = width // 2
    sections = lax.axis_size("section")
    s = lax.axis_index("section")
    j = lax.axis_index("shard")
    core = lax.rem(j, 2)
    y = lax.rem(j // 2, RING)
    x = j // (2 * RING)

    def device(px, py, pc):
        return (px * RING + py) * 2 + pc

    xp = device(lax.rem(x + 1, RING), y, core)
    xm = device(lax.rem(x + RING - 1, RING), y, core)
    yp = device(x, lax.rem(y + 1, RING), core)
    ym = device(x, lax.rem(y + RING - 1, RING), core)
    targets = {
        "a+": xp * (1 - core) + yp * core,
        "a-": xm * (1 - core) + ym * core,
        "b+": yp * (1 - core) + xp * core,
        "b-": ym * (1 - core) + xm * core,
        "s": device(x, y, 1 - core),
    }
    copies = plane_copies()
    numbers = {name: at for at, name in enumerate(copies)}

    loads = [
        pltpu.make_async_copy(deltas.at[0], inp.at[0], in_sem.at[0]),
        pltpu.make_async_copy(backs.at[0], inp.at[1], in_sem.at[1]),
    ]
    for load in loads:
        load.start()

    barrier = pltpu.get_barrier_semaphore()
    for target in targets.values():
        pl.semaphore_signal(barrier, device_id=(s, target), device_id_type=pl.DeviceIdType.MESH)
    for step in (1, sections - 1):
        pl.semaphore_signal(
            barrier, device_id=(lax.rem(s + step, sections), j), device_id_type=pl.DeviceIdType.MESH
        )
    pl.semaphore_wait(barrier, len(targets) + 2)
    for load in loads:
        load.wait()

    def copy(t, m, name):
        source, landing, half, target = copies[name]
        at = numbers[name]
        src, dst = g.at[t, m, source], g.at[t, m, landing]
        if half is not None:
            columns = pl.ds(half * half_width, half_width)
            src, dst = src.at[:, columns], dst.at[:, columns]
        return pltpu.make_async_remote_copy(
            src_ref=src,
            dst_ref=dst,
            send_sem=send.at[t, m, at],
            recv_sem=recv.at[t, m, at],
            device_id=(s, targets[target]),
            device_id_type=pl.DeviceIdType.MESH,
        )

    def z_copy(t, m, c):
        return pltpu.make_async_remote_copy(
            src_ref=zbuf.at[t, m, c],
            dst_ref=zbuf.at[t, m, c],
            send_sem=zsend.at[t, m, c],
            recv_sem=zrecv.at[t, m, c],
            device_id=(lax.rem(s + 1 - 2 * t + sections, sections), j),
            device_id_type=pl.DeviceIdType.MESH,
        )

    early = s // (sections // 2)
    middle = ((s == sections // 2) | (s == sections // 2 - 1)).astype(jnp.int32)
    total = 2 * CHUNKS

    def place(t):
        return s * (1 - t) + (sections - 1 - s) * t

    @pl.loop(0, 2 * total)
    def _(e):
        order_apart = e // total
        chunk_apart = lax.rem(e, total)
        lead = 2
        inside = ((e >= lead) & (e < 2 * total - lead)).astype(jnp.int32)
        after = e // (2 * total - lead)
        order_mixed = inside * lax.rem(e, 2) + after
        chunk_mixed = (
            inside * ((1 - lax.rem(e, 2)) * ((e + lead) // 2) + lax.rem(e, 2) * ((e - lead) // 2))
            + after * (e - total)
            + (1 - inside) * (1 - after) * e
        )
        order = middle * order_mixed + (1 - middle) * order_apart
        chunk = middle * chunk_mixed + (1 - middle) * chunk_apart
        t = early + order - 2 * early * order
        m = chunk // CHUNKS
        c = lax.rem(chunk, CHUNKS)
        at = place(t)
        columns = pl.ds(pl.multiple_of(c * part, part), part)

        @pl.when(at > 0)
        def _():
            z_copy(t, m, c).wait_recv()
            zbuf[t, m, c] = zbuf[t, m, c] + inp[t, m, :, columns].astype(jnp.float32)

        @pl.when(at == 0)
        def _():
            zbuf[t, m, c] = inp[t, m, :, columns].astype(jnp.float32)

        @pl.when(at < sections - 1)
        def _():
            z_copy(t, m, c).start()

        @pl.when((c == CHUNKS - 1) & (t == 0))
        def _():
            squares = jnp.zeros((8, 1), jnp.float32)
            for k in range(CHUNKS):
                f = zbuf[0, m, k]
                squares = squares + jnp.sum(f * f, axis=-1, keepdims=True)
            inverse = lax.rsqrt(squares / width + EPSILON)
            for k in range(CHUNKS):
                spot = pl.ds(k * part, part)
                f = zbuf[0, m, k]
                g[0, m, 0, :, spot] = (f * inverse * gains[:, spot]).astype(jnp.bfloat16)

        @pl.when((c == CHUNKS - 1) & (t == 1))
        def _():
            for k in range(CHUNKS):
                g[1, m, 0, :, pl.ds(k * part, part)] = zbuf[1, m, k].astype(jnp.bfloat16)

        @pl.when(c == CHUNKS - 1)
        def _():
            for name in (("a+", 0), ("a-", 0), ("b+", 0, 0), ("b-", 0, 0), ("s", 0)):
                copy(t, m, name).start()

    @pl.loop(0, 4)
    def _(u):
        order = u // 2
        t = early + order - 2 * early * order
        m = lax.rem(u, 2)

        def arrived(*name):
            copy(t, m, name).wait_recv()

        def go(*name):
            copy(t, m, name).start()

        arrived("a+", 0)
        go("a+", 1)
        go("b+", 3, 0)
        go("b-", 3, 0)
        go("s", slot(3, 0))
        arrived("a-", 0)
        go("a-", 1)
        go("b+", 1, 0)
        go("b-", 1, 0)
        go("s", slot(1, 0))
        arrived("b+", 0, 0)
        go("b+", 0, 1)
        go("s", slot(0, 3))
        arrived("b-", 0, 0)
        go("b-", 0, 1)
        go("s", slot(0, 1))
        arrived("a+", 1)
        arrived("a-", 1)
        go("b+", 2, 0)
        go("b-", 2, 0)
        go("s", slot(2, 0))
        for da in (3, 1, 2):
            arrived("b+", da, 0)
            go("b+", da, 1)
            go("s", slot(da, 3))
            arrived("b-", da, 0)
            go("b-", da, 1)
            go("s", slot(da, 1))
        for da in ORDER:
            arrived("b+", da, 1)
            arrived("b-", da, 1)
            go("s", slot(da, 2))

    @pl.loop(0, 4)
    def _(u):
        t = u // 2
        m = lax.rem(u, 2)
        for at in range(PLANE):
            copy(t, m, ("s", at)).wait_recv()
        for name in copies:
            copy(t, m, name).wait_send()

        @pl.when(place(t) < sections - 1)
        def _():
            for c in range(CHUNKS):
                z_copy(t, m, c).wait_send()


def gathered(deltas, backs, gains):
    _, micro, rows, width = deltas.shape
    return pl.pallas_call(
        gather_kernel,
        out_shape=pltpu.VMEM((2, micro, 2 * PLANE, rows, width), jnp.bfloat16),
        in_specs=[
            pl.BlockSpec(memory_space=pl.ANY),
            pl.BlockSpec(memory_space=pl.ANY),
            pl.BlockSpec(memory_space=pltpu.VMEM),
        ],
        out_specs=pl.BlockSpec(memory_space=pltpu.VMEM),
        scratch_shapes=[
            pltpu.VMEM((2, micro, rows, width), jnp.bfloat16),
            pltpu.VMEM((2, micro, CHUNKS, rows, width // CHUNKS), jnp.float32),
            pltpu.SemaphoreType.DMA((2,)),
            pltpu.SemaphoreType.DMA((2, micro, CHUNKS)),
            pltpu.SemaphoreType.DMA((2, micro, CHUNKS)),
            pltpu.SemaphoreType.DMA((2, micro, SENDS)),
            pltpu.SemaphoreType.DMA((2, micro, SENDS)),
        ],
        compiler_params=pltpu.CompilerParams(
            collective_id=0, has_side_effects=True, vmem_limit_bytes=40 * 2**20
        ),
        name="gather",
    )(deltas, backs, gains)


def shards(deltas, backs, gains):
    width = deltas.shape[-1]
    tile_rows = width // lax.axis_size("shard")
    own_start = lax.axis_index("shard") * tile_rows
    g = gathered(deltas, backs, gains)
    tokens = g.shape[1] * g.shape[2] * g.shape[3]
    contract = (((0,), (0,)), ((), ()))
    outs = []
    for t in range(2):
        rows = g[t].reshape(tokens, width)
        left = lax.dynamic_slice_in_dim(rows, own_start, tile_rows, 1)
        full = lax.dot_general(left, rows, contract, preferred_element_type=jnp.float32)
        outs.append((full / tokens).astype(jnp.bfloat16)[None])
    return tuple(outs)


def solution(mesh):
    return jax.shard_map(
        shards,
        mesh=mesh,
        in_specs=(
            P("section", None, "shard", None),
            P("section", None, "shard", None),
            P("section", None),
        ),
        out_specs=(P("section", "shard", None), P("section", "shard", None)),
        check_vma=False,
    )
```

time: 174 us -> 122 us (0.70)
  the two profiles are of different devices: /device:TPU:97 before, /device:TPU:1 now
where the time goes in v1:
time: 122 us
  Pallas kernels  102 us (84%)
  matrix products  12.6 us (10%)
  local copies, waits for them, and re-layouts  6.18 us (5%)
    pallas_call x1, Pallas kernels, gathered(): pl.pallas_call(gather_kernel, out_shape=pltpu.VMEM((2, micro, 2 * PLANE,...  102 us
    dot_general x2, matrix products, shards(): lax.dot_general(left, rows, contract, preferred_element_type=jnp.float32)  12.6 us
    slice x1, local copies, waits for them, and re-layouts, shards(): rows = g[t].reshape(tokens, width)  6.17 us

profile of v1, /device:TPU:1, one launch (start us, length us, event | category | flops | bytes accessed | tf_op | source)
XLA Modules:
  0.0 121.5 jit_solution(5805557377673676466)
XLA Ops:
  0.6 102.1 %gather.1 = bf16[2,2,32,8,8192]{4,3,2,1,0:T(8,128)(2,1)S(1)} custom-call(bf16[1,2,8,8192]{3,2,1,0:T(8,128)(2,1)} %deltas.1, bf16[1,2,8,8192]{3,2,1,0:T(8,128)(2,1)} %backs.1, f32[1,8192]{1,0:T(1,128)} %gains.1), custom_call_target="tpu_custom_call" | custom-call | tf_op jit(solution)/shard_map/gather/pallas_call | solution.py:234
  102.8 6.2 %fusion.8 = (bf16[1,2,32,8,8192]{4,3,2,1,0:T(8,128)(2,1)}, bf16[1,2,32,8,8192]{4,3,2,1,0:T(8,128)(2,1)}) fusion(bf16[2,2,32,8,8192]{4,3,2,1,0:T(8,128)(2,1)S(1)} %gather.1), kind=kLoop, calls=%fused_computation.10 | loop fusion | bytes 33554432 | tf_op jit(solution)/shard_map/slice | solution.py:268
  108.9 0.0 copy-start
  108.9 8.0 %fusion.3 = bf16[1,256,8192]{2,1,0:T(8,128)(2,1)} fusion(bf16[512,8192]{1,0:T(8,128)(2,1)} %bitcast.9, s32[]{:T(128)S(6)} %select_n.4), kind=kOutput, calls=%fused_computation.5 | convolution fusion | flops 2151677952 | bytes 12845060 | tf_op jit(solution)/shard_map/dot_general | solution.py:270
  117.0 0.0 copy-done
  117.0 4.5 %fusion.2 = bf16[1,256,8192]{2,1,0:T(8,128)(2,1)} fusion(bf16[512,8192]{1,0:T(8,128)(2,1)S(1)} %bitcast.8, s32[]{:T(128)S(6)} %select_n.4), kind=kOutput, calls=%fused_computation.4 | convolution fusion | flops 2151677952 | bytes 12845060 | tf_op jit(solution)/shard_map/dot_general | solution.py:270
Async XLA Ops:
  108.9 8.0 %copy-start = (bf16[1,2,32,8,8192]{4,3,2,1,0:T(8,128)(2,1)S(1)}, bf16[1,2,32,8,8192]{4,3,2,1,0:T(8,128)(2,1)}, u32[]{:S(2)}) copy-start(bf16[1,2,32,8,8192]{4,3,2,1,0:T(8,128)(2,1)} %get-tuple-element.2) | copy-start | bytes 25165828

commit v2 on v1

--- a/solution.py
+++ b/solution.py
@@ -12,6 +12,7 @@
 PLANE = RING * RING
 SENDS = 36
 ORDER = (0, 3, 1, 2)
+BLOCK = 1024
 
 
 def slot(da, db):
@@ -34,7 +35,7 @@
     return copies
 
 
-def gather_kernel(deltas, backs, gains, g, inp, zbuf, in_sem, zsend, zrecv, send, recv):
+def gather_kernel(deltas, backs, gains_in, g, inp, gains, zbuf, in_sem, zsend, zrecv, send, recv):
     width = inp.shape[-1]
     part = width // CHUNKS
     half_width = width // 2
@@ -65,6 +66,7 @@
     loads = [
         pltpu.make_async_copy(deltas.at[0], inp.at[0], in_sem.at[0]),
         pltpu.make_async_copy(backs.at[0], inp.at[1], in_sem.at[1]),
+        pltpu.make_async_copy(gains_in, gains, in_sem.at[2]),
     ]
     for load in loads:
         load.start()
@@ -113,8 +115,7 @@
     def place(t):
         return s * (1 - t) + (sections - 1 - s) * t
 
-    @pl.loop(0, 2 * total)
-    def _(e):
+    def z_event(e):
         order_apart = e // total
         chunk_apart = lax.rem(e, total)
         lead = 2
@@ -169,8 +170,7 @@
             for name in (("a+", 0), ("a-", 0), ("b+", 0, 0), ("b-", 0, 0), ("s", 0)):
                 copy(t, m, name).start()
 
-    @pl.loop(0, 4)
-    def _(u):
+    def unit(u):
         order = u // 2
         t = early + order - 2 * early * order
         m = lax.rem(u, 2)
@@ -181,38 +181,86 @@
         def go(*name):
             copy(t, m, name).start()
 
+        return arrived, go
+
+    def stage_1(u):
+        arrived, go = unit(u)
         arrived("a+", 0)
         go("a+", 1)
         go("b+", 3, 0)
         go("b-", 3, 0)
-        go("s", slot(3, 0))
         arrived("a-", 0)
         go("a-", 1)
         go("b+", 1, 0)
         go("b-", 1, 0)
-        go("s", slot(1, 0))
         arrived("b+", 0, 0)
         go("b+", 0, 1)
-        go("s", slot(0, 3))
         arrived("b-", 0, 0)
         go("b-", 0, 1)
-        go("s", slot(0, 1))
+        for at in (slot(3, 0), slot(1, 0), slot(0, 3), slot(0, 1)):
+            go("s", at)
+
+    def stage_2(u):
+        arrived, go = unit(u)
         arrived("a+", 1)
         arrived("a-", 1)
         go("b+", 2, 0)
         go("b-", 2, 0)
         go("s", slot(2, 0))
-        for da in (3, 1, 2):
+        for da in (3, 1):
             arrived("b+", da, 0)
             go("b+", da, 1)
-            go("s", slot(da, 3))
             arrived("b-", da, 0)
             go("b-", da, 1)
+            go("s", slot(da, 3))
             go("s", slot(da, 1))
+
+    def stage_3(u):
+        arrived, go = unit(u)
+        arrived("b+", 2, 0)
+        go("b+", 2, 1)
+        arrived("b-", 2, 0)
+        go("b-", 2, 1)
+        go("s", slot(2, 3))
+        go("s", slot(2, 1))
+
+    def stage_4(u):
+        arrived, go = unit(u)
         for da in ORDER:
             arrived("b+", da, 1)
             arrived("b-", da, 1)
             go("s", slot(da, 2))
+
+    stages = (stage_1, stage_2, stage_3, stage_4)
+    near = jnp.minimum(s, sections - 1 - s)
+    outer = (near == 0).astype(jnp.int32) * 2
+    ahead = (
+        outer + ((near == 1) | (near == 2)).astype(jnp.int32),
+        outer + (near == 1).astype(jnp.int32),
+        outer,
+        outer,
+    )
+    split = total * (1 + middle)
+
+    @pl.loop(0, split)
+    def _(e):
+        z_event(e)
+
+    for stage, count in zip(stages, ahead):
+
+        @pl.loop(0, count)
+        def _(u):
+            stage(u)
+
+    @pl.loop(split, 2 * total)
+    def _(e):
+        z_event(e)
+
+    for stage, count in zip(stages, ahead):
+
+        @pl.loop(count, 4)
+        def _(u):
+            stage(u)
 
     @pl.loop(0, 4)
     def _(u):
@@ -237,13 +285,14 @@
         in_specs=[
             pl.BlockSpec(memory_space=pl.ANY),
             pl.BlockSpec(memory_space=pl.ANY),
-            pl.BlockSpec(memory_space=pltpu.VMEM),
+            pl.BlockSpec(memory_space=pl.ANY),
         ],
         out_specs=pl.BlockSpec(memory_space=pltpu.VMEM),
         scratch_shapes=[
             pltpu.VMEM((2, micro, rows, width), jnp.bfloat16),
+            pltpu.VMEM((1, width), jnp.float32),
             pltpu.VMEM((2, micro, CHUNKS, rows, width // CHUNKS), jnp.float32),
-            pltpu.SemaphoreType.DMA((2,)),
+            pltpu.SemaphoreType.DMA((3,)),
             pltpu.SemaphoreType.DMA((2, micro, CHUNKS)),
             pltpu.SemaphoreType.DMA((2, micro, CHUNKS)),
             pltpu.SemaphoreType.DMA((2, micro, SENDS)),
@@ -256,20 +305,61 @@
     )(deltas, backs, gains)
 
 
+def covariance_kernel(g, act, grad, left, rows, sem):
+    _, micro, slots, low, width = g.shape
+    tokens = micro * slots * low
+    tile = left.shape[1]
+    steps = width // BLOCK
+    start = pl.multiple_of(lax.axis_index("shard") * tile, tile)
+    outs = (act, grad)
+    for t in range(2):
+        own = g[t, :, :, :, pl.ds(start, tile)].reshape(tokens, tile)
+        left[t] = own.T
+
+    def block(step):
+        return pl.ds(pl.multiple_of(step * BLOCK, BLOCK), BLOCK)
+
+    def write(t, step):
+        at = lax.rem(step, 2)
+        return pltpu.make_async_copy(rows.at[t, at], outs[t].at[0, :, block(step)], sem.at[t, at])
+
+    @pl.loop(0, steps)
+    def _(step):
+        for t in range(2):
+
+            @pl.when(step > 1)
+            def _():
+                write(t, step - 2).wait()
+
+            right = g[t, :, :, :, block(step)].reshape(tokens, BLOCK)
+            full = jnp.dot(left[t], right, preferred_element_type=jnp.float32)
+            rows[t, lax.rem(step, 2)] = (full / tokens).astype(jnp.bfloat16)
+            write(t, step).start()
+
+    for t in range(2):
+        for step in (steps - 2, steps - 1):
+            write(t, step).wait()
+
+
 def shards(deltas, backs, gains):
     width = deltas.shape[-1]
-    tile_rows = width // lax.axis_size("shard")
-    own_start = lax.axis_index("shard") * tile_rows
+    tile = width // lax.axis_size("shard")
     g = gathered(deltas, backs, gains)
     tokens = g.shape[1] * g.shape[2] * g.shape[3]
-    contract = (((0,), (0,)), ((), ()))
-    outs = []
-    for t in range(2):
-        rows = g[t].reshape(tokens, width)
-        left = lax.dynamic_slice_in_dim(rows, own_start, tile_rows, 1)
-        full = lax.dot_general(left, rows, contract, preferred_element_type=jnp.float32)
-        outs.append((full / tokens).astype(jnp.bfloat16)[None])
-    return tuple(outs)
+    out = jax.ShapeDtypeStruct((1, tile, width), jnp.bfloat16)
+    return pl.pallas_call(
+        covariance_kernel,
+        out_shape=(out, out),
+        in_specs=[pl.BlockSpec(memory_space=pltpu.VMEM)],
+        out_specs=(pl.BlockSpec(memory_space=pl.ANY), pl.BlockSpec(memory_space=pl.ANY)),
+        scratch_shapes=[
+            pltpu.VMEM((2, tile, tokens), jnp.bfloat16),
+            pltpu.VMEM((2, 2, tile, BLOCK), jnp.bfloat16),
+            pltpu.SemaphoreType.DMA((2, 2)),
+        ],
+        compiler_params=pltpu.CompilerParams(vmem_limit_bytes=24 * 2**20),
+        name="covariance",
+    )(pltpu.with_memory_space_constraint(g, pltpu.VMEM))
 
 
 def solution(mesh):

time: 122 us -> 79.8 us (0.65)
  the two profiles are of different devices: /device:TPU:1 before, /device:TPU:97 now
where the time goes in v2:
time: 79.8 us; the launch traced here: 78.7 us
  Pallas kernels  78.1 us (98%)
    pallas_call x1, Pallas kernels, gathered(): pl.pallas_call(gather_kernel, out_shape=pltpu.VMEM((2, micro, 2 * PLANE,...  69.9 us
    pallas_call x1, Pallas kernels, shards(): pl.pallas_call(covariance_kernel, out_shape=(out, out), in_specs=[pl.Bloc...  8.13 us

profile of v2, /device:TPU:97, one launch (start us, length us, event | category | flops | bytes accessed | tf_op | source)
XLA Modules:
  0.0 78.7 jit_solution(4815614220195044825)
XLA Ops:
  0.6 69.9 %gather.1.g = bf16[2,2,32,8,8192]{4,3,2,1,0:T(8,128)(2,1)S(1)} custom-call(bf16[1,2,8,8192]{3,2,1,0:T(8,128)(2,1)} %deltas.1, bf16[1,2,8,8192]{3,2,1,0:T(8,128)(2,1)} %backs.1, f32[1,8192]{1,0:T(1,128)} %gains_in.1), custom_call_target="tpu_custom_call" | custom-call | tf_op jit(solution)/shard_map/gather/pallas_call | solution.py:282
  70.6 8.1 %covariance.1 = (bf16[1,256,8192]{2,1,0:T(8,128)(2,1)}, bf16[1,256,8192]{2,1,0:T(8,128)(2,1)}) custom-call(bf16[2,2,32,8,8192]{4,3,2,1,0:T(8,128)(2,1)S(1)} %gather.1.g), custom_call_target="tpu_custom_call" | custom-call | tf_op jit(solution)/shard_map/covariance/pallas_call | solution.py:350

commit v3 on v2

--- a/solution.py
+++ b/solution.py
@@ -7,16 +7,39 @@
 from jax.sharding import PartitionSpec as P
 
 EPSILON = 1e-05
-CHUNKS = 4
+CHUNKS = 8
+LEAD = 4
 RING = 4
 PLANE = RING * RING
 SENDS = 36
 ORDER = (0, 3, 1, 2)
-BLOCK = 1024
+BLOCK = 4096
+Z_ENDS = ((16, 16, 21, 22), (16, 19, 31, 31), (16, 22, 31, 31), (30, 32, 31, 31), (32, 32, 32, 32))
+STAGE_ENDS = (
+    ((1, 1, 1, 1), (2, 1, 1, 2), (2, 2, 1, 2), (2, 2, 1, 2)),
+    ((1, 0, 0, 0), (1, 1, 1, 0), (2, 1, 1, 0), (2, 1, 1, 0)),
+    ((0, 0, 0, 0), (1, 0, 0, 0), (2, 0, 0, 0), (2, 1, 0, 0)),
+    ((0, 0, 0, 0), (0, 0, 0, 0), (0, 0, 0, 0), (1, 0, 0, 0)),
+)
+
+
+GROUPS = (
+    ((0, 0), (3, 0), (1, 0), (0, 3), (0, 1), (2, 0), (3, 3), (3, 1)),
+    ((1, 3), (1, 1), (2, 3), (2, 1), (0, 2), (3, 2), (1, 2), (2, 2)),
+)
+GROUP_ENDS = (16, 32)
 
 
 def slot(da, db):
-    return da * RING + db
+    start = 0
+    for group in GROUPS:
+        if (da, db) in group:
+            return start + group.index((da, db))
+        start += 2 * len(group)
+
+
+def other(at):
+    return at + len(GROUPS[0])
 
 
 def plane_copies():
@@ -30,14 +53,30 @@
         copies["b-", da, 0] = (slot(da, 0), slot(da, 1), None, "b-")
         copies["b+", da, 1] = (slot(da, 3), slot(da, 2), 0, "b+")
         copies["b-", da, 1] = (slot(da, 1), slot(da, 2), 1, "b-")
-    for at in range(PLANE):
-        copies["s", at] = (at, PLANE + at, None, "s")
+    for group in GROUPS:
+        for place in group:
+            at = slot(*place)
+            copies["s", at] = (at, other(at), None, "s")
     return copies
 
 
-def gather_kernel(deltas, backs, gains_in, g, inp, gains, zbuf, in_sem, zsend, zrecv, send, recv):
+def tokens_of(g, t, group, columns):
+    start = GROUP_ENDS[group - 1] if group else 0
+    rows = g[t, :, start : GROUP_ENDS[group], :, columns]
+    return rows.reshape(rows.shape[0] * rows.shape[1] * rows.shape[2], rows.shape[3])
+
+
+def own_columns(tile):
+    return pl.ds(pl.multiple_of(lax.axis_index("shard") * tile, tile), tile)
+
+
+def block_columns(step):
+    return pl.ds(pl.multiple_of(step * BLOCK, BLOCK), BLOCK)
+
+
+def gather_kernel(deltas, backs, gains_in, g, part, inp, gains, zbuf, in_sem, zsend, zrecv, send, recv):
     width = inp.shape[-1]
-    part = width // CHUNKS
+    piece = width // CHUNKS
     half_width = width // 2
     sections = lax.axis_size("section")
     s = lax.axis_index("section")
@@ -118,7 +157,7 @@
     def z_event(e):
         order_apart = e // total
         chunk_apart = lax.rem(e, total)
-        lead = 2
+        lead = LEAD
         inside = ((e >= lead) & (e < 2 * total - lead)).astype(jnp.int32)
         after = e // (2 * total - lead)
         order_mixed = inside * lax.rem(e, 2) + after
@@ -133,7 +172,7 @@
         m = chunk // CHUNKS
         c = lax.rem(chunk, CHUNKS)
         at = place(t)
-        columns = pl.ds(pl.multiple_of(c * part, part), part)
+        columns = pl.ds(pl.multiple_of(c * piece, piece), piece)
 
         @pl.when(at > 0)
         def _():
@@ -156,14 +195,14 @@
                 squares = squares + jnp.sum(f * f, axis=-1, keepdims=True)
             inverse = lax.rsqrt(squares / width + EPSILON)
             for k in range(CHUNKS):
-                spot = pl.ds(k * part, part)
+                spot = pl.ds(k * piece, piece)
                 f = zbuf[0, m, k]
                 g[0, m, 0, :, spot] = (f * inverse * gains[:, spot]).astype(jnp.bfloat16)
 
         @pl.when((c == CHUNKS - 1) & (t == 1))
         def _():
             for k in range(CHUNKS):
-                g[1, m, 0, :, pl.ds(k * part, part)] = zbuf[1, m, k].astype(jnp.bfloat16)
+                g[1, m, 0, :, pl.ds(k * piece, piece)] = zbuf[1, m, k].astype(jnp.bfloat16)
 
         @pl.when(c == CHUNKS - 1)
         def _():
@@ -233,61 +272,99 @@
 
     stages = (stage_1, stage_2, stage_3, stage_4)
     near = jnp.minimum(s, sections - 1 - s)
-    outer = (near == 0).astype(jnp.int32) * 2
-    ahead = (
-        outer + ((near == 1) | (near == 2)).astype(jnp.int32),
-        outer + (near == 1).astype(jnp.int32),
-        outer,
-        outer,
-    )
-    split = total * (1 + middle)
-
-    @pl.loop(0, split)
-    def _(e):
-        z_event(e)
-
-    for stage, count in zip(stages, ahead):
-
-        @pl.loop(0, count)
-        def _(u):
-            stage(u)
-
-    @pl.loop(split, 2 * total)
-    def _(e):
-        z_event(e)
-
-    for stage, count in zip(stages, ahead):
-
-        @pl.loop(count, 4)
-        def _(u):
-            stage(u)
+
+    def pick(values):
+        return sum(value * (near == at).astype(jnp.int32) for at, value in enumerate(values))
+
+    def run(stage, since, ends, permuted=True):
+        @pl.loop(pick(since), pick(ends))
+        def _(rank):
+            swap = (rank == 1).astype(jnp.int32) - (rank == 2).astype(jnp.int32)
+            stage(rank + middle * swap if permuted else rank)
+
+    def add_up(order, group):
+        t = early + order - 2 * early * order
+        for m in range(2):
+            for place in GROUPS[group]:
+                copy(t, m, ("s", slot(*place))).wait_recv()
+        left = tokens_of(g, t, group, own_columns(part.shape[1])).T
+
+        @pl.loop(0, width // BLOCK)
+        def _(step):
+            columns = block_columns(step)
+            more = jnp.dot(
+                left, tokens_of(g, t, group, columns), preferred_element_type=jnp.float32
+            )
+            part[t, :, columns] = part[t, :, columns] + more if group else more
+
+    before = (0, 0, 0, 0)
+    for segment, ends in enumerate(Z_ENDS):
+        if ends != before:
+
+            @pl.loop(pick(before), pick(ends))
+            def _(e):
+                z_event(e)
+
+        before = ends
+        if segment == len(Z_ENDS) - 1:
+            break
+        for stage, table in zip(stages, STAGE_ENDS):
+            since = table[segment - 1] if segment else (0, 0, 0, 0)
+            if table[segment] != since:
+                run(stage, since, table[segment])
+
+    since_1, since_2, since_3, since_4 = (table[-1] for table in STAGE_ENDS)
+    three, four = (3, 3, 3, 3), (4, 4, 4, 4)
+    run(stage_1, since_1, four)
+    run(stage_2, since_2, three)
+    add_up(0, 0)
+    run(stage_2, three, four)
+    run(stage_3, since_3, three)
+    add_up(1, 0)
+    run(stage_3, three, four)
+
+    late = [("s", slot(da, 2)) for da in ORDER]
+    rest = [("s", slot(*spot)) for spot in GROUPS[1]]
 
     @pl.loop(0, 4)
     def _(u):
         t = u // 2
         m = lax.rem(u, 2)
-        for at in range(PLANE):
-            copy(t, m, ("s", at)).wait_recv()
         for name in copies:
-            copy(t, m, name).wait_send()
+            if name not in late:
+                copy(t, m, name).wait_send()
 
         @pl.when(place(t) < sections - 1)
         def _():
             for c in range(CHUNKS):
                 z_copy(t, m, c).wait_send()
+
+    run(stage_4, since_4, four, permuted=False)
+
+    @pl.loop(0, 4)
+    def _(u):
+        t = u // 2
+        m = lax.rem(u, 2)
+        for name in rest:
+            copy(t, m, name).wait_recv()
+        for name in late:
+            copy(t, m, name).wait_send()
 
 
 def gathered(deltas, backs, gains):
     _, micro, rows, width = deltas.shape
     return pl.pallas_call(
         gather_kernel,
-        out_shape=pltpu.VMEM((2, micro, 2 * PLANE, rows, width), jnp.bfloat16),
+        out_shape=(
+            pltpu.VMEM((2, micro, 2 * PLANE, rows, width), jnp.bfloat16),
+            pltpu.VMEM((2, width // lax.axis_size("shard"), width), jnp.float32),
+        ),
         in_specs=[
-            pl.BlockSpec(memory_space=pl.ANY),
-            pl.BlockSpec(memory_space=pl.ANY),
-            pl.BlockSpec(memory_space=pl.ANY),
+            pl.BlockSpec(memory_space=pltpu.HBM),
+            pl.BlockSpec(memory_space=pltpu.HBM),
+            pl.BlockSpec(memory_space=pltpu.HBM),
         ],
-        out_specs=pl.BlockSpec(memory_space=pltpu.VMEM),
+        out_specs=(pl.BlockSpec(memory_space=pltpu.VMEM), pl.BlockSpec(memory_space=pltpu.VMEM)),
         scratch_shapes=[
             pltpu.VMEM((2, micro, rows, width), jnp.bfloat16),
             pltpu.VMEM((1, width), jnp.float32),
@@ -299,29 +376,27 @@
             pltpu.SemaphoreType.DMA((2, micro, SENDS)),
         ],
         compiler_params=pltpu.CompilerParams(
-            collective_id=0, has_side_effects=True, vmem_limit_bytes=40 * 2**20
+            collective_id=0, has_side_effects=True, vmem_limit_bytes=20 * 2**20
         ),
         name="gather",
-    )(deltas, backs, gains)
-
-
-def covariance_kernel(g, act, grad, left, rows, sem):
+    )(*(pltpu.with_memory_space_constraint(a, pltpu.HBM) for a in (deltas, backs, gains)))
+
+
+def covariance_kernel(g, part, act, grad, left, rows, sem):
     _, micro, slots, low, width = g.shape
     tokens = micro * slots * low
-    tile = left.shape[1]
+    tile = part.shape[1]
     steps = width // BLOCK
-    start = pl.multiple_of(lax.axis_index("shard") * tile, tile)
+    last = len(GROUPS) - 1
     outs = (act, grad)
     for t in range(2):
-        own = g[t, :, :, :, pl.ds(start, tile)].reshape(tokens, tile)
-        left[t] = own.T
-
-    def block(step):
-        return pl.ds(pl.multiple_of(step * BLOCK, BLOCK), BLOCK)
+        left[t] = tokens_of(g, t, last, own_columns(tile)).T
 
     def write(t, step):
         at = lax.rem(step, 2)
-        return pltpu.make_async_copy(rows.at[t, at], outs[t].at[0, :, block(step)], sem.at[t, at])
+        return pltpu.make_async_copy(
+            rows.at[t, at], outs[t].at[0, :, block_columns(step)], sem.at[t, at]
+        )
 
     @pl.loop(0, steps)
     def _(step):
@@ -331,8 +406,11 @@
             def _():
                 write(t, step - 2).wait()
 
-            right = g[t, :, :, :, block(step)].reshape(tokens, BLOCK)
-            full = jnp.dot(left[t], right, preferred_element_type=jnp.float32)
+            columns = block_columns(step)
+            right = tokens_of(g, t, last, columns)
+            full = part[t, :, columns] + jnp.dot(
+                left[t], right, preferred_element_type=jnp.float32
+            )
             rows[t, lax.rem(step, 2)] = (full / tokens).astype(jnp.bfloat16)
             write(t, step).start()
 
@@ -344,22 +422,23 @@
 def shards(deltas, backs, gains):
     width = deltas.shape[-1]
     tile = width // lax.axis_size("shard")
-    g = gathered(deltas, backs, gains)
-    tokens = g.shape[1] * g.shape[2] * g.shape[3]
+    g, part = gathered(deltas, backs, gains)
+    _, micro, slots, low, _ = g.shape
+    late_tokens = micro * low * (slots - GROUP_ENDS[-2])
     out = jax.ShapeDtypeStruct((1, tile, width), jnp.bfloat16)
     return pl.pallas_call(
         covariance_kernel,
         out_shape=(out, out),
-        in_specs=[pl.BlockSpec(memory_space=pltpu.VMEM)],
+        in_specs=[pl.BlockSpec(memory_space=pltpu.VMEM)] * 2,
         out_specs=(pl.BlockSpec(memory_space=pl.ANY), pl.BlockSpec(memory_space=pl.ANY)),
         scratch_shapes=[
-            pltpu.VMEM((2, tile, tokens), jnp.bfloat16),
+            pltpu.VMEM((2, tile, late_tokens), jnp.bfloat16),
             pltpu.VMEM((2, 2, tile, BLOCK), jnp.bfloat16),
             pltpu.SemaphoreType.DMA((2, 2)),
         ],
-        compiler_params=pltpu.CompilerParams(vmem_limit_bytes=24 * 2**20),
+        compiler_params=pltpu.CompilerParams(vmem_limit_bytes=20 * 2**20),
         name="covariance",
-    )(pltpu.with_memory_space_constraint(g, pltpu.VMEM))
+    )(*(pltpu.with_memory_space_constraint(a, pltpu.VMEM) for a in (g, part)))
 
 
 def solution(mesh):

time: 79.8 us -> 74.6 us (0.935)
  Pallas kernels: 78.1 us -> 73.1 us
    pallas_call x1, Pallas kernels: 8.13 us -> 4.36 us  [shards(): pl.pallas_call(covariance_kernel, out_shape=(out, out), in_specs=[pl.Bloc...]
    pallas_call x1, Pallas kernels: 69.9 us -> 68.8 us  [gathered(): pl.pallas_call(gather_kernel, out_shape=(pltpu.VMEM((2, micro, 2 * PLANE,...]
where the time goes in v3:
time: 74.6 us; the launch traced here: 73.8 us
  Pallas kernels  73.1 us (98%)
    pallas_call x1, Pallas kernels, gathered(): pl.pallas_call(gather_kernel, out_shape=(pltpu.VMEM((2, micro, 2 * PLANE,...  68.8 us
    pallas_call x1, Pallas kernels, shards(): pl.pallas_call(covariance_kernel, out_shape=(out, out), in_specs=[pl.Bloc...  4.36 us

profile of v3, /device:TPU:97, one launch (start us, length us, event | category | flops | bytes accessed | tf_op | source)
XLA Modules:
  0.0 73.8 jit_solution(1068821305672330448)
XLA Ops:
  0.6 68.8 %gather.1 = (bf16[2,2,32,8,8192]{4,3,2,1,0:T(8,128)(2,1)S(1)}, f32[2,256,8192]{2,1,0:T(8,128)S(1)}) custom-call(bf16[1,2,8,8192]{3,2,1,0:T(8,128)(2,1)} %deltas.1, bf16[1,2,8,8192]{3,2,1,0:T(8,128)(2,1)} %backs.1, f32[1,8192]{1,0:T(1,128)} %gains_in.1), custom_call_target="tpu_custom_call" | custom-call | tf_op jit(solution)/shard_map/gather/pallas_call | solution.py:356
  69.4 4.4 %covariance.1 = (bf16[1,256,8192]{2,1,0:T(8,128)(2,1)}, bf16[1,256,8192]{2,1,0:T(8,128)(2,1)}) custom-call(bf16[2,2,32,8,8192]{4,3,2,1,0:T(8,128)(2,1)S(1)} %get-tuple-element.4.g, f32[2,256,8192]{2,1,0:T(8,128)S(1)} %get-tuple-element.5.part), custom_call_target="tpu_custom_call" | custom-call | tf_op jit(solution)/shard_map/covariance/pallas_call | solution.py:429

commit v4 on v3

v4 whole, which is shorter than its diff:
```python
import functools
import jax
import jax.numpy as jnp
from jax import lax
from jax.experimental import pallas as pl
from jax.experimental.pallas import tpu as pltpu
from jax.sharding import PartitionSpec as P

EPSILON = 1e-05
CHUNKS = 8
LEAD = 4
RING = 4
PLANE = RING * RING
ORDER = (0, 3, 1, 2)
BLOCK = 4096
LAST_BLOCK = 2048
LANES = 128
Z_ENDS = (
    (16, 15, 13, 23, 22, 19, 16, 16),
    (16, 16, 22, 24, 22, 29, 19, 16),
    (16, 20, 30, 24, 28, 31, 21, 16),
    (30, 27, 32, 32, 31, 32, 32, 30),
    (32, 32, 32, 32, 32, 32, 32, 32),
)
STAGE_ENDS = (
    (
        (1, 1, 1, 1, 1, 1, 1, 1),
        (2, 1, 1, 1, 1, 1, 1, 2),
        (2, 2, 2, 1, 2, 1, 2, 2),
        (2, 2, 2, 2, 2, 2, 3, 2),
    ),
    (
        (1, 0, 0, 0, 0, 0, 0, 1),
        (1, 1, 1, 0, 0, 1, 1, 1),
        (2, 1, 1, 0, 0, 1, 1, 2),
        (2, 2, 2, 0, 0, 1, 1, 2),
    ),
    (
        (0, 0, 0, 0, 0, 0, 0, 0),
        (1, 0, 0, 0, 0, 0, 0, 1),
        (2, 0, 0, 0, 0, 0, 0, 2),
        (2, 1, 1, 0, 0, 1, 0, 2),
    ),
    (
        (0, 0, 0, 0, 0, 0, 0, 0),
        (0, 0, 0, 0, 0, 0, 0, 0),
        (0, 0, 0, 0, 0, 0, 0, 0),
        (1, 0, 0, 0, 0, 0, 0, 1),
    ),
)


GROUPS = (
    ((0, 0), (3, 0), (1, 0), (0, 3), (0, 1), (2, 0), (3, 3), (3, 1)),
    ((1, 3), (1, 1), (2, 3), (2, 1), (0, 2), (3, 2), (1, 2), (2, 2)),
)
GROUP_ENDS = (16, 32)


def slot(da, db):
    start = 0
    for group in GROUPS:
        if (da, db) in group:
            return start + group.index((da, db))
        start += 2 * len(group)


def other(at):
    return at + len(GROUPS[0])


AXIS, FAR, PAIR, CROSS, CORNER, SIBLING = 0, 1, 2, 6, 7, 8
WAITS = (
    (slot(3, 0), 2),
    (slot(2, 0), 1),
    (slot(0, 3), 2),
    (slot(3, 3), 2),
    (slot(1, 3), 2),
    (slot(2, 3), 2),
    (slot(0, 2), 3),
    (slot(2, 2), 1),
    (other(slot(0, 0)), 8),
    (other(slot(1, 3)), 8),
)


def unit_copies():
    copies = {
        ("a+", 0): (slot(0, 0), slot(3, 0), 1, None, "a+", AXIS),
        ("a-", 0): (slot(0, 0), slot(1, 0), 1, None, "a-", AXIS),
        ("a+", 1): (slot(3, 0), slot(2, 0), 1, 0, "a+", FAR),
        ("a-", 1): (slot(1, 0), slot(2, 0), 1, 1, "a-", FAR),
    }
    for at, da in enumerate(ORDER):
        ahead = CORNER if da == 2 else CROSS
        copies["b+", da, 0] = (slot(da, 0), slot(da, 3), 1, None, "b+", PAIR + at)
        copies["b-", da, 0] = (slot(da, 0), slot(da, 1), 1, None, "b-", PAIR + at)
        copies["b+", da, 1] = (slot(da, 3), slot(da, 2), 1, 0, "b+", ahead)
        copies["b-", da, 1] = (slot(da, 1), slot(da, 2), 1, 1, "b-", ahead)
    for place, count in (
        ((0, 0), 1),
        ((3, 0), 2),
        ((0, 3), 2),
        ((2, 0), 1),
        ((3, 3), 2),
        ((1, 3), 2),
        ((2, 3), 2),
        ((0, 2), 3),
        ((2, 2), 1),
    ):
        at = slot(*place)
        wait = SIBLING + (1 if at >= GROUP_ENDS[0] else 0)
        copies["s", place] = (at, other(at), count, None, "s", wait)
    return copies


def tokens_of(g, t, group, columns):
    start = GROUP_ENDS[group - 1] if group else 0
    rows = g[t, :, start : GROUP_ENDS[group], :, columns]
    return rows.reshape(rows.shape[0] * rows.shape[1] * rows.shape[2], rows.shape[3])


def own_columns(tile):
    return pl.ds(pl.multiple_of(lax.axis_index("shard") * tile, tile), tile)


def block_columns(step):
    return pl.ds(pl.multiple_of(step * BLOCK, BLOCK), BLOCK)


def gather_kernel(deltas, backs, gains_in, g, part, inp, gains, zbuf, squares, in_sem, zsend, zrecv, send, recv):
    width = inp.shape[-1]
    piece = width // CHUNKS
    half_width = width // 2
    sections = lax.axis_size("section")
    s = lax.axis_index("section")
    j = lax.axis_index("shard")
    core = lax.rem(j, 2)
    y = lax.rem(j // 2, RING)
    x = j // (2 * RING)

    def device(px, py, pc):
        return (px * RING + py) * 2 + pc

    xp = device(lax.rem(x + 1, RING), y, core)
    xm = device(lax.rem(x + RING - 1, RING), y, core)
    yp = device(x, lax.rem(y + 1, RING), core)
    ym = device(x, lax.rem(y + RING - 1, RING), core)
    targets = {
        "a+": xp * (1 - core) + yp * core,
        "a-": xm * (1 - core) + ym * core,
        "b+": yp * (1 - core) + xp * core,
        "b-": ym * (1 - core) + xm * core,
        "s": device(x, y, 1 - core),
    }
    copies = unit_copies()

    loads = [
        pltpu.make_async_copy(deltas.at[0], inp.at[0], in_sem.at[0]),
        pltpu.make_async_copy(backs.at[0], inp.at[1], in_sem.at[1]),
        pltpu.make_async_copy(gains_in, gains, in_sem.at[2]),
    ]
    for load in loads:
        load.start()

    barrier = pltpu.get_barrier_semaphore()
    for target in targets.values():
        pl.semaphore_signal(barrier, device_id=(s, target), device_id_type=pl.DeviceIdType.MESH)
    for step in (1, sections - 1):
        pl.semaphore_signal(
            barrier, device_id=(lax.rem(s + step, sections), j), device_id_type=pl.DeviceIdType.MESH
        )
    pl.semaphore_wait(barrier, len(targets) + 2)
    for load in loads:
        load.wait()

    def copy(t, m, name):
        source, landing, count, half, target, wait = copies[name]
        src, dst = g.at[t, m, pl.ds(source, count)], g.at[t, m, pl.ds(landing, count)]
        if half is not None:
            columns = pl.ds(half * half_width, half_width)
            src, dst = src.at[:, :, columns], dst.at[:, :, columns]
        return pltpu.make_async_remote_copy(
            src_ref=src,
            dst_ref=dst,
            send_sem=send.at[t, m],
            recv_sem=recv.at[t, m, wait],
            device_id=(s, targets[target]),
            device_id_type=pl.DeviceIdType.MESH,
        )

    def whole(t, m, start, count, wait):
        places = g.at[t, m, pl.ds(start, count)]
        return pltpu.make_async_remote_copy(
            src_ref=places,
            dst_ref=places,
            send_sem=send.at[t, m],
            recv_sem=recv.at[t, m, wait],
            device_id=(s, targets["s"]),
            device_id_type=pl.DeviceIdType.MESH,
        )

    def take(t, m, wait):
        whole(t, m, *WAITS[wait], wait).wait_recv()

    def z_copy(t, m, c):
        return pltpu.make_async_remote_copy(
            src_ref=zbuf.at[t, m, c],
            dst_ref=zbuf.at[t, m, c],
            send_sem=zsend.at[t],
            recv_sem=zrecv.at[t, m, c],
            device_id=(lax.rem(s + 1 - 2 * t + sections, sections), j),
            device_id_type=pl.DeviceIdType.MESH,
        )

    early = s // (sections // 2)
    middle = ((s == sections // 2) | (s == sections // 2 - 1)).astype(jnp.int32)
    total = 2 * CHUNKS

    def place(t):
        return s * (1 - t) + (sections - 1 - s) * t

    def z_event(e):
        order_apart = e // total
        chunk_apart = lax.rem(e, total)
        lead = LEAD
        inside = ((e >= lead) & (e < 2 * total - lead)).astype(jnp.int32)
        after = e // (2 * total - lead)
        order_mixed = inside * lax.rem(e, 2) + after
        chunk_mixed = (
            inside * ((1 - lax.rem(e, 2)) * ((e + lead) // 2) + lax.rem(e, 2) * ((e - lead) // 2))
            + after * (e - total)
            + (1 - inside) * (1 - after) * e
        )
        order = middle * order_mixed + (1 - middle) * order_apart
        chunk = middle * chunk_mixed + (1 - middle) * chunk_apart
        t = early + order - 2 * early * order
        m = chunk // CHUNKS
        c = lax.rem(chunk, CHUNKS)
        at = place(t)
        columns = pl.ds(pl.multiple_of(c * piece, piece), piece)

        @pl.when(at > 0)
        def _():
            z_copy(t, m, c).wait_recv()
            zbuf[t, m, c] = zbuf[t, m, c] + inp[t, m, :, columns].astype(jnp.float32)

        @pl.when(at == 0)
        def _():
            zbuf[t, m, c] = inp[t, m, :, columns].astype(jnp.float32)

        @pl.when(at < sections - 1)
        def _():
            z_copy(t, m, c).start()

        @pl.when(t == 0)
        def _():
            f = zbuf[0, m, c]
            f = f * f
            more = sum(f[:, k : k + LANES] for k in range(0, piece, LANES))
            squares[m] = jnp.where(c == 0, 0.0, squares[m]) + more

        @pl.when(t == 1)
        def _():
            g[1, m, 0, :, columns] = zbuf[1, m, c].astype(jnp.bfloat16)

        @pl.when((c == CHUNKS - 1) & (t == 0))
        def _():
            total_square = jnp.sum(squares[m], axis=-1, keepdims=True)
            inverse = lax.rsqrt(total_square / width + EPSILON)
            for k in range(CHUNKS):
                spot = pl.ds(k * piece, piece)
                g[0, m, 0, :, spot] = (zbuf[0, m, k] * inverse * gains[:, spot]).astype(
                    jnp.bfloat16
                )

        @pl.when(c == CHUNKS - 1)
        def _():
            for name in (("a+", 0), ("a-", 0), ("b+", 0, 0), ("b-", 0, 0), ("s", (0, 0))):
                copy(t, m, name).start()

    def unit(u):
        order = u // 2
        t = early + order - 2 * early * order
        m = lax.rem(u, 2)

        def arrived(wait):
            take(t, m, wait)

        def go(*names):
            for name in names:
                copy(t, m, name).start()

        return arrived, go

    def stage_1(u):
        arrived, go = unit(u)
        arrived(AXIS)
        go(("a+", 1), ("a-", 1), ("b+", 3, 0), ("b-", 3, 0), ("b+", 1, 0), ("b-", 1, 0))
        go(("s", (3, 0)))
        arrived(PAIR)
        go(("b+", 0, 1), ("b-", 0, 1), ("s", (0, 3)))

    def stage_2(u):
        arrived, go = unit(u)
        arrived(FAR)
        go(("b+", 2, 0), ("b-", 2, 0), ("s", (2, 0)))
        for at, da in enumerate(ORDER):
            if da in (1, 3):
                arrived(PAIR + at)
                go(("b+", da, 1), ("b-", da, 1), ("s", (da, 3)))

    def stage_3(u):
        arrived, go = unit(u)
        arrived(PAIR + ORDER.index(2))
        go(("b+", 2, 1), ("b-", 2, 1), ("s", (2, 3)))

    def stage_4(u):
        arrived, go = unit(u)
        arrived(CROSS)
        go(("s", (0, 2)))
        arrived(CORNER)
        go(("s", (2, 2)))

    stages = (stage_1, stage_2, stage_3, stage_4)
    def pick(values):
        return sum(value * (s == at).astype(jnp.int32) for at, value in enumerate(values))

    none = (0,) * sections

    def run(stage, since, ends, permuted=True):
        @pl.loop(pick(since), pick(ends))
        def _(rank):
            swap = (rank == 1).astype(jnp.int32) - (rank == 2).astype(jnp.int32)
            stage(rank + middle * swap if permuted else rank)

    def add_up(order, group):
        t = early + order - 2 * early * order
        for m in range(2):
            take(t, m, SIBLING + group)
        left = tokens_of(g, t, group, own_columns(part.shape[1])).T

        @pl.loop(0, width // BLOCK)
        def _(step):
            columns = block_columns(step)
            more = jnp.dot(
                left, tokens_of(g, t, group, columns), preferred_element_type=jnp.float32
            )
            part[t, :, columns] = part[t, :, columns] + more if group else more

    before = none
    for segment, ends in enumerate(Z_ENDS):
        if ends != before:

            @pl.loop(pick(before), pick(ends))
            def _(e):
                z_event(e)

        before = ends
        if segment == len(Z_ENDS) - 1:
            break
        for stage, table in zip(stages, STAGE_ENDS):
            since = table[segment - 1] if segment else none
            if table[segment] != since:
                run(stage, since, table[segment])

    since_1, since_2, since_3, since_4 = (table[-1] for table in STAGE_ENDS)
    three, four = (3,) * sections, (4,) * sections
    run(stage_1, since_1, four)
    run(stage_2, since_2, three)
    add_up(0, 0)
    run(stage_2, three, four)
    run(stage_3, since_3, three)
    add_up(1, 0)
    run(stage_3, three, four)

    run(stage_4, since_4, four, permuted=False)

    for t in range(2):
        for m in range(2):
            take(t, m, SIBLING + 1)
            whole(t, m, 0, 2 * PLANE - 1, SIBLING).wait_send()

        @pl.when(place(t) < sections - 1)
        def _():
            pltpu.make_async_remote_copy(
                src_ref=zbuf.at[t],
                dst_ref=zbuf.at[t],
                send_sem=zsend.at[t],
                recv_sem=zrecv.at[t, 0, 0],
                device_id=(lax.rem(s + 1 - 2 * t + sections, sections), j),
                device_id_type=pl.DeviceIdType.MESH,
            ).wait_send()


def gathered(deltas, backs, gains):
    _, micro, rows, width = deltas.shape
    return pl.pallas_call(
        gather_kernel,
        out_shape=(
            pltpu.VMEM((2, micro, 2 * PLANE, rows, width), jnp.bfloat16),
            pltpu.VMEM((2, width // lax.axis_size("shard"), width), jnp.float32),
        ),
        in_specs=[
            pl.BlockSpec(memory_space=pltpu.HBM),
            pl.BlockSpec(memory_space=pltpu.HBM),
            pl.BlockSpec(memory_space=pltpu.HBM),
        ],
        out_specs=(pl.BlockSpec(memory_space=pltpu.VMEM), pl.BlockSpec(memory_space=pltpu.VMEM)),
        scratch_shapes=[
            pltpu.VMEM((2, micro, rows, width), jnp.bfloat16),
            pltpu.VMEM((1, width), jnp.float32),
            pltpu.VMEM((2, micro, CHUNKS, rows, width // CHUNKS), jnp.float32),
            pltpu.VMEM((micro, rows, LANES), jnp.float32),
            pltpu.SemaphoreType.DMA((3,)),
            pltpu.SemaphoreType.DMA((2,)),
            pltpu.SemaphoreType.DMA((2, micro, CHUNKS)),
            pltpu.SemaphoreType.DMA((2, micro)),
            pltpu.SemaphoreType.DMA((2, micro, len(WAITS))),
        ],
        compiler_params=pltpu.CompilerParams(
            collective_id=0, has_side_effects=True, vmem_limit_bytes=20 * 2**20
        ),
        name="gather",
    )(*(pltpu.with_memory_space_constraint(a, pltpu.HBM) for a in (deltas, backs, gains)))


def covariance_kernel(g, part, act, grad, left, rows, sem):
    _, micro, slots, low, width = g.shape
    tokens = micro * slots * low
    tile = part.shape[1]
    last = len(GROUPS) - 1
    outs = (act, grad)
    for t in range(2):
        left[t] = tokens_of(g, t, last, own_columns(tile)).T
    writes = []
    for step in range(width // LAST_BLOCK):
        columns = pl.ds(step * LAST_BLOCK, LAST_BLOCK)
        for t in range(2):
            full = part[t, :, columns] + jnp.dot(
                left[t], tokens_of(g, t, last, columns), preferred_element_type=jnp.float32
            )
            rows[t, :, columns] = (full / tokens).astype(jnp.bfloat16)
            write = pltpu.make_async_copy(
                rows.at[t, :, columns], outs[t].at[0, :, columns], sem.at[t, step]
            )
            write.start()
            writes.append(write)
    for write in writes:
        write.wait()


def shards(deltas, backs, gains):
    width = deltas.shape[-1]
    tile = width // lax.axis_size("shard")
    g, part = gathered(deltas, backs, gains)
    _, micro, slots, low, _ = g.shape
    late_tokens = micro * low * (slots - GROUP_ENDS[-2])
    out = jax.ShapeDtypeStruct((1, tile, width), jnp.bfloat16)
    return pl.pallas_call(
        covariance_kernel,
        out_shape=(out, out),
        in_specs=[pl.BlockSpec(memory_space=pltpu.VMEM)] * 2,
        out_specs=(pl.BlockSpec(memory_space=pl.ANY), pl.BlockSpec(memory_space=pl.ANY)),
        scratch_shapes=[
            pltpu.VMEM((2, tile, late_tokens), jnp.bfloat16),
            pltpu.VMEM((2, tile, width), jnp.bfloat16),
            pltpu.SemaphoreType.DMA((2, width // LAST_BLOCK)),
        ],
        compiler_params=pltpu.CompilerParams(vmem_limit_bytes=20 * 2**20),
        name="covariance",
    )(*(pltpu.with_memory_space_constraint(a, pltpu.VMEM) for a in (g, part)))


def solution(mesh):
    return jax.shard_map(
        shards,
        mesh=mesh,
        in_specs=(
            P("section", None, "shard", None),
            P("section", None, "shard", None),
            P("section", None),
        ),
        out_specs=(P("section", "shard", None), P("section", "shard", None)),
        check_vma=False,
    )
```

time: 74.6 us -> 71.8 us (0.962)
  Pallas kernels: 73.1 us -> 70.2 us
    pallas_call x1, Pallas kernels: 68.8 us -> 66.3 us  [gathered(): pl.pallas_call(gather_kernel, out_shape=(pltpu.VMEM((2, micro, 2 * PLANE,...]
where the time goes in v4:
time: 71.8 us; the launch traced here: 70.8 us
  Pallas kernels  70.2 us (98%)
    pallas_call x1, Pallas kernels, gathered(): pl.pallas_call(gather_kernel, out_shape=(pltpu.VMEM((2, micro, 2 * PLANE,...  66.3 us
    pallas_call x1, Pallas kernels, shards(): pl.pallas_call(covariance_kernel, out_shape=(out, out), in_specs=[pl.Bloc...  3.86 us

profile of v4, /device:TPU:97, one launch (start us, length us, event | category | flops | bytes accessed | tf_op | source)
XLA Modules:
  0.0 70.8 jit_solution(16693660011902507428)
XLA Ops:
  0.6 66.3 %gather.1 = (bf16[2,2,32,8,8192]{4,3,2,1,0:T(8,128)(2,1)S(1)}, f32[2,256,8192]{2,1,0:T(8,128)S(1)}) custom-call(bf16[1,2,8,8192]{3,2,1,0:T(8,128)(2,1)} %deltas.1, bf16[1,2,8,8192]{3,2,1,0:T(8,128)(2,1)} %backs.1, f32[1,8192]{1,0:T(1,128)} %gains_in.1), custom_call_target="tpu_custom_call" | custom-call | tf_op jit(solution)/shard_map/gather/pallas_call | solution.py:398
  67.0 3.9 %covariance.1 = (bf16[1,256,8192]{2,1,0:T(8,128)(2,1)}, bf16[1,256,8192]{2,1,0:T(8,128)(2,1)}) custom-call(bf16[2,2,32,8,8192]{4,3,2,1,0:T(8,128)(2,1)S(1)} %get-tuple-element.4.g, f32[2,256,8192]{2,1,0:T(8,128)S(1)} %get-tuple-element.5.part), custom_call_target="tpu_custom_call" | custom-call | tf_op jit(solution)/shard_map/covariance/pallas_call | solution.py:460

commit v5 on v4

--- a/solution.py
+++ b/solution.py
@@ -7,8 +7,8 @@
 from jax.sharding import PartitionSpec as P
 
 EPSILON = 1e-05
-CHUNKS = 8
-LEAD = 4
+CHUNKS = 16
+LEADS = (8, 4)
 RING = 4
 PLANE = RING * RING
 ORDER = (0, 3, 1, 2)
@@ -16,24 +16,24 @@
 LAST_BLOCK = 2048
 LANES = 128
 Z_ENDS = (
-    (16, 15, 13, 23, 22, 19, 16, 16),
-    (16, 16, 22, 24, 22, 29, 19, 16),
-    (16, 20, 30, 24, 28, 31, 21, 16),
-    (30, 27, 32, 32, 31, 32, 32, 30),
-    (32, 32, 32, 32, 32, 32, 32, 32),
+    (32, 30, 38, 46, 44, 38, 32, 32),
+    (32, 32, 58, 48, 44, 58, 38, 32),
+    (32, 40, 62, 48, 56, 62, 42, 32),
+    (60, 54, 64, 64, 62, 64, 64, 60),
+    (64, 64, 64, 64, 64, 64, 64, 64),
 )
 STAGE_ENDS = (
     (
         (1, 1, 1, 1, 1, 1, 1, 1),
         (2, 1, 1, 1, 1, 1, 1, 2),
-        (2, 2, 2, 1, 2, 1, 2, 2),
+        (2, 2, 1, 1, 2, 1, 2, 2),
         (2, 2, 2, 2, 2, 2, 3, 2),
     ),
     (
         (1, 0, 0, 0, 0, 0, 0, 1),
         (1, 1, 1, 0, 0, 1, 1, 1),
         (2, 1, 1, 0, 0, 1, 1, 2),
-        (2, 2, 2, 0, 0, 1, 1, 2),
+        (2, 2, 1, 0, 0, 1, 1, 2),
     ),
     (
         (0, 0, 0, 0, 0, 0, 0, 0),
@@ -166,11 +166,16 @@
     barrier = pltpu.get_barrier_semaphore()
     for target in targets.values():
         pl.semaphore_signal(barrier, device_id=(s, target), device_id_type=pl.DeviceIdType.MESH)
-    for step in (1, sections - 1):
-        pl.semaphore_signal(
-            barrier, device_id=(lax.rem(s + step, sections), j), device_id_type=pl.DeviceIdType.MESH
-        )
-    pl.semaphore_wait(barrier, len(targets) + 2)
+    above, below = (s < sections - 1).astype(jnp.int32), (s > 0).astype(jnp.int32)
+    for there, step in ((above, 1), (below, -1)):
+
+        @pl.when(there == 1)
+        def _():
+            pl.semaphore_signal(
+                barrier, device_id=(s + step, j), device_id_type=pl.DeviceIdType.MESH
+            )
+
+    pl.semaphore_wait(barrier, len(targets) + above + below)
     for load in loads:
         load.wait()
 
@@ -223,9 +228,9 @@
     def z_event(e):
         order_apart = e // total
         chunk_apart = lax.rem(e, total)
-        lead = LEAD
+        lead = LEADS[0] * (1 - early) + LEADS[1] * early
         inside = ((e >= lead) & (e < 2 * total - lead)).astype(jnp.int32)
-        after = e // (2 * total - lead)
+        after = (e >= 2 * total - lead).astype(jnp.int32)
         order_mixed = inside * lax.rem(e, 2) + after
         chunk_mixed = (
             inside * ((1 - lax.rem(e, 2)) * ((e + lead) // 2) + lax.rem(e, 2) * ((e - lead) // 2))

time: 71.8 us -> 72.9 us (1.015)
  Pallas kernels: 70.2 us -> 71.3 us
    pallas_call x1, Pallas kernels: 66.3 us -> 67.5 us  [gathered(): pl.pallas_call(gather_kernel, out_shape=(pltpu.VMEM((2, micro, 2 * PLANE,...]
where the time goes in v5:
time: 72.9 us; the launch traced here: 72 us
  Pallas kernels  71.3 us (98%)
    pallas_call x1, Pallas kernels, gathered(): pl.pallas_call(gather_kernel, out_shape=(pltpu.VMEM((2, micro, 2 * PLANE,...  67.5 us
    pallas_call x1, Pallas kernels, shards(): pl.pallas_call(covariance_kernel, out_shape=(out, out), in_specs=[pl.Bloc...  3.86 us

profile of v5, /device:TPU:97, one launch (start us, length us, event | category | flops | bytes accessed | tf_op | source)
XLA Modules:
  0.0 72.0 jit_solution(16444568101232498856)
XLA Ops:
  0.6 67.5 %gather.1 = (bf16[2,2,32,8,8192]{4,3,2,1,0:T(8,128)(2,1)S(1)}, f32[2,256,8192]{2,1,0:T(8,128)S(1)}) custom-call(bf16[1,2,8,8192]{3,2,1,0:T(8,128)(2,1)} %deltas.1, bf16[1,2,8,8192]{3,2,1,0:T(8,128)(2,1)} %backs.1, f32[1,8192]{1,0:T(1,128)} %gains_in.1), custom_call_target="tpu_custom_call" | custom-call | tf_op jit(solution)/shard_map/gather/pallas_call | solution.py:403
  68.1 3.9 %covariance.1 = (bf16[1,256,8192]{2,1,0:T(8,128)(2,1)}, bf16[1,256,8192]{2,1,0:T(8,128)(2,1)}) custom-call(bf16[2,2,32,8,8192]{4,3,2,1,0:T(8,128)(2,1)S(1)} %get-tuple-element.4.g, f32[2,256,8192]{2,1,0:T(8,128)S(1)} %get-tuple-element.5.part), custom_call_target="tpu_custom_call" | custom-call | tf_op jit(solution)/shard_map/covariance/pallas_call | solution.py:465

commit v6 on v5

--- a/solution.py
+++ b/solution.py
@@ -8,7 +8,7 @@
 
 EPSILON = 1e-05
 CHUNKS = 16
-LEADS = (8, 4)
+LEADS = (12, 12)
 RING = 4
 PLANE = RING * RING
 ORDER = (0, 3, 1, 2)

time: 72.9 us -> 70.3 us (0.964); the launches traced: 72 us -> 70.2 us
  Pallas kernels: 71.3 us -> 69.6 us
    pallas_call x1, Pallas kernels: 67.5 us -> 65.7 us  [gathered(): pl.pallas_call(gather_kernel, out_shape=(pltpu.VMEM((2, micro, 2 * PLANE,...]
where the time goes in v6:
time: 70.3 us; the launch traced here: 70.2 us
  Pallas kernels  69.6 us (99%)
    pallas_call x1, Pallas kernels, gathered(): pl.pallas_call(gather_kernel, out_shape=(pltpu.VMEM((2, micro, 2 * PLANE,...  65.7 us
    pallas_call x1, Pallas kernels, shards(): pl.pallas_call(covariance_kernel, out_shape=(out, out), in_specs=[pl.Bloc...  3.86 us

profile of v6, /device:TPU:97, one launch (start us, length us, event | category | flops | bytes accessed | tf_op | source)
XLA Modules:
  0.0 70.2 jit_solution(2156595618206491361)
XLA Ops:
  0.6 65.7 %gather.1 = (bf16[2,2,32,8,8192]{4,3,2,1,0:T(8,128)(2,1)S(1)}, f32[2,256,8192]{2,1,0:T(8,128)S(1)}) custom-call(bf16[1,2,8,8192]{3,2,1,0:T(8,128)(2,1)} %deltas.1, bf16[1,2,8,8192]{3,2,1,0:T(8,128)(2,1)} %backs.1, f32[1,8192]{1,0:T(1,128)} %gains_in.1), custom_call_target="tpu_custom_call" | custom-call | tf_op jit(solution)/shard_map/gather/pallas_call | solution.py:403
  66.4 3.9 %covariance.1 = (bf16[1,256,8192]{2,1,0:T(8,128)(2,1)}, bf16[1,256,8192]{2,1,0:T(8,128)(2,1)}) custom-call(bf16[2,2,32,8,8192]{4,3,2,1,0:T(8,128)(2,1)S(1)} %get-tuple-element.4.g, f32[2,256,8192]{2,1,0:T(8,128)S(1)} %get-tuple-element.5.part), custom_call_target="tpu_custom_call" | custom-call | tf_op jit(solution)/shard_map/covariance/pallas_call | solution.py:465

commit v7 on v6

--- a/solution.py
+++ b/solution.py
@@ -13,7 +13,7 @@
 PLANE = RING * RING
 ORDER = (0, 3, 1, 2)
 BLOCK = 4096
-LAST_BLOCK = 2048
+LAST_BLOCK = 1024
 LANES = 128
 Z_ENDS = (
     (32, 30, 38, 46, 44, 38, 32, 32),
@@ -375,9 +375,8 @@
     run(stage_2, since_2, three)
     add_up(0, 0)
     run(stage_2, three, four)
-    run(stage_3, since_3, three)
+    run(stage_3, since_3, four)
     add_up(1, 0)
-    run(stage_3, three, four)
 
     run(stage_4, since_4, four, permuted=False)
 

time: 70.3 us -> 70.2 us (level)
  no operation moved by 1% of the time
where the time goes in v7:
time: 70.2 us; the launch traced here: 70.1 us
  Pallas kernels  69.5 us (99%)
    pallas_call x1, Pallas kernels, gathered(): pl.pallas_call(gather_kernel, out_shape=(pltpu.VMEM((2, micro, 2 * PLANE,...  65.7 us
    pallas_call x1, Pallas kernels, shards(): pl.pallas_call(covariance_kernel, out_shape=(out, out), in_specs=[pl.Bloc...  3.77 us

profile of v7, /device:TPU:97, one launch (start us, length us, event | category | flops | bytes accessed | tf_op | source)
XLA Modules:
  0.0 70.1 jit_solution(1135182182881033948)
XLA Ops:
  0.6 65.7 %gather.1 = (bf16[2,2,32,8,8192]{4,3,2,1,0:T(8,128)(2,1)S(1)}, f32[2,256,8192]{2,1,0:T(8,128)S(1)}) custom-call(bf16[1,2,8,8192]{3,2,1,0:T(8,128)(2,1)} %deltas.1, bf16[1,2,8,8192]{3,2,1,0:T(8,128)(2,1)} %backs.1, f32[1,8192]{1,0:T(1,128)} %gains_in.1), custom_call_target="tpu_custom_call" | custom-call | tf_op jit(solution)/shard_map/gather/pallas_call | solution.py:402
  66.4 3.8 %covariance.1 = (bf16[1,256,8192]{2,1,0:T(8,128)(2,1)}, bf16[1,256,8192]{2,1,0:T(8,128)(2,1)}) custom-call(bf16[2,2,32,8,8192]{4,3,2,1,0:T(8,128)(2,1)S(1)} %get-tuple-element.4.g, f32[2,256,8192]{2,1,0:T(8,128)S(1)} %get-tuple-element.5.part), custom_call_target="tpu_custom_call" | custom-call | tf_op jit(solution)/shard_map/covariance/pallas_call | solution.py:464
